TPU v7x, 256 devices: a whole 4x4x8 slice. The times are simulated.
256 devices in a mesh: rows: 8 (over x, core), protos: 32 (over y, z).
Axes of the slice: x: 4, y: 4, z: 8, core: 2. Of those that a mesh axis runs over, the one named last changes fastest.
Arguments:
- teacher_features: bfloat16 [4096, 384], P(('rows', 'protos')), may hold values from -80 to 80, as said below
- student_features: bfloat16 [4096, 384], P(('rows', 'protos')), may hold values from -80 to 80, as said below
- prototypes: bfloat16 [131072, 384], P('protos'), may hold values from -80 to 80, as said below
Outputs:
- feature_grad: float32 [4096, 384], P(('rows', 'protos'))
- proto_grad: float32 [8, 16384, 384], P('rows', 'protos')
Inputs may be any that keep to these rules, and one draw needn't show every extreme that they name: `teacher_features`: every row has nonzero entries. `student_features`: every row has nonzero entries. `prototypes`: every row has nonzero entries.
All inputs are finite; a program needn't handle non-finite values.
Results may differ from a plain program's by a relative error of at most 0.012.
The roundings to bfloat16 on the way count: a program that leaves them out, or rounds other values in their place, can miss the bound.
Values may be sent and summed in bfloat16 or wider, within the bound.
A program may use at most 64 MiB of HBM per device.

v0:
```python
import math
import jax
import jax.numpy as jnp
from jax import lax
from jax.sharding import PartitionSpec as P

D = 384
K = 131072
PASSES = 3
eps = 1e-06


def unitize(values):
    values = values.astype(jnp.float32)
    return (values * lax.rsqrt(jnp.sum(values * values, axis=1, keepdims=True) + eps)).astype(
        jnp.bfloat16
    )


def against(left, right):
    return lax.dot_general(
        left, right, (((1,), (1,)), ((), ())), preferred_element_type=jnp.float32
    )


def on_device(teacher_features, student_features, prototypes):
    scale = 1.5 * math.sqrt(D)
    unit_w = unitize(prototypes)
    local_t = unitize(teacher_features)
    local_s = unitize(student_features)
    unit_t, unit_s = (
        lax.all_gather(local_t, "protos", axis=0, tiled=True),
        lax.all_gather(local_s, "protos", axis=0, tiled=True),
    )
    kernel = jnp.exp(scale * against(unit_t, unit_w))
    powers = jnp.exp(scale * against(unit_s, unit_w))
    student_part = jnp.sum(powers, axis=1)
    student_whole = lax.psum(student_part, "protos")
    row_scale = jnp.ones((kernel.shape[0],), jnp.float32)
    col_scale = jnp.ones((kernel.shape[1],), jnp.float32)
    for step in range(PASSES):
        col_part = jnp.dot(row_scale, kernel, precision=lax.Precision.HIGHEST)
        col_scale = 1.0 / lax.psum(col_part, "rows")
        row_part = jnp.dot(kernel, col_scale, precision=lax.Precision.HIGHEST)
        if step == 0:
            row_whole = lax.psum(row_part, "protos")
        else:
            row_whole = lax.psum(row_part, "protos")
        row_scale = 1.0 / row_whole
    target = kernel * row_scale[:, None] * col_scale[None, :]
    probs = powers / student_whole[:, None]
    delta = (probs - target).astype(jnp.bfloat16)
    feature_term = scale * jnp.dot(delta, unit_w, preferred_element_type=jnp.float32)
    feature_grad = lax.psum_scatter(feature_term, "protos", scatter_dimension=0, tiled=True)
    row_groups = lax.axis_size("rows")
    total_rows = delta.shape[0] * row_groups
    factor = scale * K / total_rows
    block = delta.shape[1] // row_groups
    term = factor * lax.dot_general(
        delta, unit_s, (((0,), (0,)), ((), ())), preferred_element_type=jnp.float32
    )
    proto_grad = lax.psum_scatter(
        term.reshape(row_groups, block, term.shape[1]), "rows", scatter_dimension=0, tiled=True
    )
    return (feature_grad, proto_grad)


def solution(mesh):
    return jax.shard_map(
        on_device,
        mesh=mesh,
        in_specs=(P(("rows", "protos"), None), P(("rows", "protos"), None), P("protos", None)),
        out_specs=(P(("rows", "protos"), None), P("rows", "protos", None)),
        check_vma=False,
    )
```

profile of v0, /device:TPU:1, one launch (start us, length us, event | category | flops | bytes accessed | tf_op | source)
XLA Modules:
  0.0 735.6 jit_solution(5828482277272511359)
XLA Ops:
  7.2 0.0 reduce-scatter.3.cloned.1.call-start
  7.2 0.8 fusion.5
  8.0 0.8 fusion.3
  8.9 0.8 fusion.4
  9.7 0.8 fusion.6
  10.4 2.6 fusion.1
  13.0 0.0 copy-start.3
  13.1 41.6 %all_gather.6 = bf16[512,384]{1,0:T(8,128)(2,1)S(1)} all-gather(bf16[16,384]{1,0:T(8,128)(2,1)S(1)} %fusion.4), channel_id=1, replica_groups=mesh['rows'=8,'protos'=32] {'protos'}, dimensions={0}, use_global_device_ids=true | all-gather | bytes 405504 | tf_op jit(solution)/shard_map/all_gather | solution.py:33
  54.6 36.7 %all_gather.7 = bf16[512,384]{1,0:T(8,128)(2,1)S(1)} all-gather(bf16[16,384]{1,0:T(8,128)(2,1)S(1)} %fusion.6), channel_id=1, replica_groups=mesh['rows'=8,'protos'=32] {'protos'}, dimensions={0}, use_global_device_ids=true | all-gather | bytes 405504 | tf_op jit(solution)/shard_map/all_gather | solution.py:32
  91.3 4.3 multiply_exponential_fusion
  95.7 0.0 copy-start
  95.7 3.2 copy-done
  98.9 4.0 fusion.7
  102.9 0.0 copy-done.3
  102.9 44.7 %psum.50 = f32[4096]{0:T(1024)S(1)} all-reduce(f32[4096]{0:T(1024)S(1)} %bitcast.34), channel_id=1, replica_groups=mesh['rows'=8,'protos'=32] {'rows'}, use_global_device_ids=true, to_apply=%region_5.0 | all-reduce | flops 4096 | bytes 32768 | tf_op jit(solution)/shard_map/psum | solution.py:43
  147.7 9.4 %fusion.14 = f32[1,512]{1,0:T(1,128)S(1)} fusion(f32[512,4096]{1,0:T(8,128)} %copy-done, f32[4096,1]{0,1:T(1,128)S(1)} %bitcast.30), kind=kOutput, calls=%fused_computation.31 | convolution fusion | flops 25165824 | bytes 8407040 | tf_op jit(solution)/shard_map/dot_general | solution.py:44
  157.1 58.6 %psum.51 = f32[512]{0:T(512)S(1)} all-reduce(f32[512]{0:T(512)S(1)} %bitcast.36), channel_id=1, replica_groups=mesh['rows'=8,'protos'=32] {'protos'}, use_global_device_ids=true, to_apply=%region_6.0 | all-reduce | flops 512 | bytes 4096 | tf_op jit(solution)/shard_map/psum | solution.py:46
  215.7 6.3 fusion.15
  222.1 37.4 %psum.52 = f32[4096]{0:T(1024)S(1)} all-reduce(f32[4096]{0:T(1024)S(1)} %bitcast.31), channel_id=1, replica_groups=mesh['rows'=8,'protos'=32] {'rows'}, use_global_device_ids=true, to_apply=%region_7.0 | all-reduce | flops 4096 | bytes 32768 | tf_op jit(solution)/shard_map/psum | solution.py:43
  259.5 9.4 %fusion.16 = f32[1,512]{1,0:T(1,128)S(1)} fusion(f32[512,4096]{1,0:T(8,128)} %copy-done, f32[4096,1]{0,1:T(1,128)S(1)} %bitcast.32), kind=kOutput, calls=%fused_computation.33 | convolution fusion | flops 25165824 | bytes 8407040 | tf_op jit(solution)/shard_map/dot_general | solution.py:44
  268.9 55.8 %psum.53 = f32[512]{0:T(512)S(1)} all-reduce(f32[512]{0:T(512)S(1)} %bitcast.38), channel_id=1, replica_groups=mesh['rows'=8,'protos'=32] {'protos'}, use_global_device_ids=true, to_apply=%region_8.0 | all-reduce | flops 512 | bytes 4096 | tf_op jit(solution)/shard_map/psum | solution.py:48
  324.7 0.0 copy-start.1
  324.7 6.5 fusion.17
  331.2 37.6 %psum.54 = f32[4096]{0:T(1024)} all-reduce(f32[4096]{0:T(1024)S(1)} %bitcast.33), channel_id=1, replica_groups=mesh['rows'=8,'protos'=32] {'rows'}, use_global_device_ids=true, to_apply=%region_9.0 | all-reduce | flops 4096 | bytes 32768 | tf_op jit(solution)/shard_map/psum | solution.py:43
  368.8 0.7 broadcast_divide_fusion
  369.6 10.0 %fusion.18 = f32[1,512]{1,0:T(1,128)} fusion(f32[512,4096]{1,0:T(8,128)} %copy-done, f32[4096,1]{0,1:T(1,128)S(1)} %bitcast.29), kind=kOutput, calls=%fused_computation.35 | convolution fusion | flops 25165824 | bytes 8407040 | tf_op jit(solution)/shard_map/dot_general | solution.py:44
  379.6 0.0 copy-done.1
  379.6 6.2 fusion
  385.8 58.2 %all-reduce = (f32[512]{0:T(512)}, f32[512]{0:T(512)}) all-reduce(f32[512]{0:T(512)} %bitcast.35, f32[512]{0:T(512)} %get-tuple-element.4), channel_id=1, replica_groups=mesh['rows'=8,'protos'=32] {'protos'}, use_global_device_ids=true, to_apply=%region_10.0 | all-reduce | flops 1024 | bytes 8192 | tf_op jit(solution)/shard_map/psum | solution.py:48
  444.0 0.7 broadcast_divide_fusion.5
  444.6 0.0 copy-start.4
  444.6 7.3 subtract_convert_fusion
  452.0 0.0 copy-start.2
  452.0 2.0 copy-done.2
  454.0 0.0 copy-done.4
  454.0 3.3 convolution_multiply_fusion.1
  457.4 0.0 reduce-scatter.3.cloned.1.call-update
  457.4 0.0 reduce-scatter.5.cloned.1.call-start
  457.4 7.2 convolution_multiply_fusion
  464.7 0.0 reduce-scatter.5.cloned.1.call-update
  464.7 212.9 %reduce-scatter.3.cloned.1.call-done = f32[16,384]{1,0:T(8,128)} async-done(((f32[512,384]{1,0:T(8,128)}), f32[16,384]{1,0:T(8,128)}) %reduce-scatter.3.cloned.1.call-update) | async-done | bytes 24592 | tf_op jit(solution)/shard_map/reduce_scatter | solution.py:54
  677.6 51.2 %reduce-scatter.5.cloned.1.call-done = f32[1,512,384]{2,1,0:T(8,128)} async-done(((f32[8,512,384]{2,1,0:T(8,128)}), f32[1,512,384]{2,1,0:T(8,128)}) %reduce-scatter.5.cloned.1.call-update) | async-done | bytes 786448 | tf_op jit(solution)/shard_map/reduce_scatter | solution.py:62
  (7 shorter events, 0.0 us)
Async XLA Ops:
  7.2 670.4 %reduce-scatter.3.cloned.1.call-start = ((), (), s32[]{:S(2)}) async-start(), calls=%async_computation.2 | async-start | bytes 811008 | tf_op jit(solution)/shard_map/reduce_scatter | solution.py:54
  13.0 89.9 %copy-start.3 = (f32[4096]{0:T(1024)}, f32[4096]{0:T(1024)S(1)}, u32[]{:S(2)}) copy-start(f32[4096]{0:T(1024)S(1)} %add_rsqrt_fusion) | copy-start | bytes 49156
  95.7 3.2 copy-start
  324.7 54.9 %copy-start.1 = (bf16[4096,384]{1,0:T(8,128)(2,1)S(1)}, bf16[4096,384]{1,0:T(8,128)(2,1)}, u32[]{:S(2)}) copy-start(bf16[4096,384]{1,0:T(8,128)(2,1)} %param.5) | copy-start | bytes 9437188
  444.6 9.4 %copy-start.4 = (f32[4096]{0:T(1024)S(1)}, f32[4096]{0:T(1024)}, u32[]{:S(2)}) copy-start(f32[4096]{0:T(1024)} %copy-done.3) | copy-start | bytes 49156
  452.0 2.0 copy-start.2
  457.4 271.4 %reduce-scatter.5.cloned.1.call-start = ((), (), s32[]{:S(2)}) async-start(), calls=%async_computation.3 | async-start | bytes 7077888 | tf_op jit(solution)/shard_map/reduce_scatter | solution.py:62
Sparse Core Ops, SparseCore 0:
  457.5 220.0 reduce-scatter.2
  680.7 48.0 reduce-scatter.4
where the time goes:
time: 736 us
  blocking collectives  371 us (50%)
  waiting for transfers between devices  264 us (36%)
  matrix products  66.9 us (9%)
  other arithmetic  14.6 us (2%)
  between operations  14.1 us (2%)
    reduce_scatter x1, waiting for transfers between devices, on_device(): lax.psum_scatter(feature_term, 'protos', scatter_dimension=0, tiled=True)  213 us
    psum x3, blocking collectives, on_device(): row_whole = lax.psum(row_part, 'protos')  173 us
    psum x3, blocking collectives, on_device(): col_scale = 1.0 / lax.psum(col_part, 'rows')  120 us
    reduce_scatter x1, waiting for transfers between devices, on_device(): lax.psum_scatter(term.reshape(row_groups, block, term.shape[1]), 'rows',...  51.2 us
    all_gather x1, blocking collectives, on_device(): lax.all_gather(local_s, 'protos', axis=0, tiled=True)  41.6 us
    all_gather x1, blocking collectives, on_device(): lax.all_gather(local_t, 'protos', axis=0, tiled=True)  36.7 us
    dot_general x3, matrix products, on_device(): row_part = jnp.dot(kernel, col_scale, precision=lax.Precision.HIGHEST)  28.9 us
    dot_general x3, matrix products, on_device(): col_part = jnp.dot(row_scale, kernel, precision=lax.Precision.HIGHEST)  16.9 us
  transfers between devices with their start and end apart: 2, of which 2 were waited for; matrix products, arithmetic and copies ran while one was open for 1% of the time, Pallas kernels for 0%

commit v1 on v0

--- a/solution.py
+++ b/solution.py
@@ -8,6 +8,11 @@
 K = 131072
 PASSES = 3
 eps = 1e-06
+
+
+def gather_by_exchange(x, axis, dim):
+    copies = jnp.concatenate([x] * lax.axis_size(axis), axis=dim)
+    return lax.all_to_all(copies, axis, dim, dim, tiled=True)
 
 
 def unitize(values):
@@ -30,7 +35,7 @@
     local_s = unitize(student_features)
     unit_t, unit_s = (
         lax.all_gather(local_t, "protos", axis=0, tiled=True),
-        lax.all_gather(local_s, "protos", axis=0, tiled=True),
+        gather_by_exchange(local_s, "protos", 0),
     )
     kernel = jnp.exp(scale * against(unit_t, unit_w))
     powers = jnp.exp(scale * against(unit_s, unit_w))

time: 736 us -> 743 us (level)
  blocking collectives: 371 us -> 319 us
  other arithmetic: 14.6 us -> 57.9 us
  starting transfers between devices: 0.08 us -> 12.1 us
    unnamed x0 -> x31, other arithmetic: none -> 42.7 us
    all_gather x1 -> x0, blocking collectives: 41.6 us -> none  [on_device(): lax.all_gather(local_s, 'protos', axis=0, tiled=True)]
    all_to_all x0 -> x1, starting transfers between devices: none -> 12 us  [gather_by_exchange(): return lax.all_to_all(copies, axis, dim, dim, tiled=True)]
    psum x3, blocking collectives: 120 us -> 108 us  [on_device(): col_scale = 1.0 / lax.psum(col_part, 'rows')]
  transfers between devices with their start and end apart: 2 -> 3, of which waited for: 2 -> 2; matrix products, arithmetic and copies ran while one was open for 1% -> 8% of each run, Pallas kernels for 0% -> 0%
where the time goes in v1:
time: 743 us; the launch traced here: 740 us
  blocking collectives  319 us (43%)
  waiting for transfers between devices  264 us (36%)
  matrix products  66.9 us (9%)
  other arithmetic  57.9 us (8%)
  between operations  14.1 us (2%)
  starting transfers between devices  12.1 us (2%)
    reduce_scatter x1, waiting for transfers between devices, on_device(): lax.psum_scatter(feature_term, 'protos', scatter_dimension=0, tiled=True)  213 us
    psum x3, blocking collectives, on_device(): row_whole = lax.psum(row_part, 'protos')  173 us
    psum x3, blocking collectives, on_device(): col_scale = 1.0 / lax.psum(col_part, 'rows')  108 us
    reduce_scatter x1, waiting for transfers between devices, on_device(): lax.psum_scatter(term.reshape(row_groups, block, term.shape[1]), 'rows',...  51.1 us
    unnamed x31, other arithmetic  42.7 us
    all_gather x1, blocking collectives, on_device(): lax.all_gather(local_t, 'protos', axis=0, tiled=True)  38.8 us
    dot_general x3, matrix products, on_device(): row_part = jnp.dot(kernel, col_scale, precision=lax.Precision.HIGHEST)  28.9 us
    dot_general x3, matrix products, on_device(): col_part = jnp.dot(row_scale, kernel, precision=lax.Precision.HIGHEST)  16.9 us
  transfers between devices with their start and end apart: 3, of which 2 were waited for; matrix products, arithmetic and copies ran while one was open for 8% of the time, Pallas kernels for 0%

profile of v1, /device:TPU:1, one launch (start us, length us, event | category | flops | bytes accessed | tf_op | source)
XLA Modules:
  0.0 739.6 jit_solution(3998740801087864482)
XLA Ops:
  8.0 1.4 constant_dynamic-update-slice_fusion.31
  13.5 1.4 constant_dynamic-update-slice_fusion.27
  14.9 1.4 constant_dynamic-update-slice_fusion.26
  16.3 1.4 constant_dynamic-update-slice_fusion.25
  17.7 1.4 constant_dynamic-update-slice_fusion.24
  19.0 1.4 constant_dynamic-update-slice_fusion.23
  20.4 1.4 constant_dynamic-update-slice_fusion.22
  21.8 1.4 constant_dynamic-update-slice_fusion.21
  23.2 1.4 constant_dynamic-update-slice_fusion.20
  24.5 1.4 constant_dynamic-update-slice_fusion.19
  25.9 1.4 constant_dynamic-update-slice_fusion.18
  27.3 1.4 constant_dynamic-update-slice_fusion.17
  28.7 1.4 constant_dynamic-update-slice_fusion.16
  30.1 1.4 constant_dynamic-update-slice_fusion.15
  31.4 1.4 constant_dynamic-update-slice_fusion.14
  39.7 1.4 constant_dynamic-update-slice_fusion.8
  41.1 1.4 constant_dynamic-update-slice_fusion.7
  42.5 1.4 constant_dynamic-update-slice_fusion.6
  43.8 1.4 constant_dynamic-update-slice_fusion.5
  45.2 1.4 constant_dynamic-update-slice_fusion.4
  46.6 1.4 constant_dynamic-update-slice_fusion.3
  48.0 1.4 constant_dynamic-update-slice_fusion.2
  49.4 1.4 constant_dynamic-update-slice_fusion.1
  50.7 1.4 constant_dynamic-update-slice_fusion
  52.1 12.0 %all-to-all-start = ((bf16[32,16,384]{2,1,0:T(8,128)(2,1)}), bf16[32,16,384]{2,1,0:T(8,128)(2,1)S(1)}, u32[]{:S(2)}, u32[]{:S(2)}) async-start(bf16[32,16,384]{2,1,0:T(8,128)(2,1)} %bitcast), calls=%async_computation | async-start | bytes 786432 | tf_op jit(solution)/shard_map/all_to_all | solution.py:15
  65.8 2.6 fusion.1
  68.4 38.8 %all_gather.3 = bf16[512,384]{1,0:T(8,128)(2,1)S(1)} all-gather(bf16[16,384]{1,0:T(8,128)(2,1)S(1)} %fusion.6), channel_id=1, replica_groups=mesh['rows'=8,'protos'=32] {'protos'}, dimensions={0}, use_global_device_ids=true | all-gather | bytes 405504 | tf_op jit(solution)/shard_map/all_gather | solution.py:37
  107.2 4.3 multiply_exponential_fusion
  111.5 3.2 copy-done
  114.8 4.0 fusion.7
  118.8 32.9 %psum.50 = f32[4096]{0:T(1024)S(1)} all-reduce(f32[4096]{0:T(1024)S(1)} %bitcast.38), channel_id=1, replica_groups=mesh['rows'=8,'protos'=32] {'rows'}, use_global_device_ids=true, to_apply=%region_5.0 | all-reduce | flops 4096 | bytes 32768 | tf_op jit(solution)/shard_map/psum | solution.py:48
  151.7 9.4 %fusion.14 = f32[1,512]{1,0:T(1,128)S(1)} fusion(f32[512,4096]{1,0:T(8,128)} %copy-done, f32[4096,1]{0,1:T(1,128)S(1)} %bitcast.34), kind=kOutput, calls=%fused_computation.63 | convolution fusion | flops 25165824 | bytes 8407040 | tf_op jit(solution)/shard_map/dot_general | solution.py:49
  161.2 58.6 %psum.51 = f32[512]{0:T(512)S(1)} all-reduce(f32[512]{0:T(512)S(1)} %bitcast.40), channel_id=1, replica_groups=mesh['rows'=8,'protos'=32] {'protos'}, use_global_device_ids=true, to_apply=%region_6.0 | all-reduce | flops 512 | bytes 4096 | tf_op jit(solution)/shard_map/psum | solution.py:51
  219.8 6.3 fusion.15
  226.1 37.4 %psum.52 = f32[4096]{0:T(1024)S(1)} all-reduce(f32[4096]{0:T(1024)S(1)} %bitcast.35), channel_id=1, replica_groups=mesh['rows'=8,'protos'=32] {'rows'}, use_global_device_ids=true, to_apply=%region_7.0 | all-reduce | flops 4096 | bytes 32768 | tf_op jit(solution)/shard_map/psum | solution.py:48
  263.6 9.4 %fusion.16 = f32[1,512]{1,0:T(1,128)S(1)} fusion(f32[512,4096]{1,0:T(8,128)} %copy-done, f32[4096,1]{0,1:T(1,128)S(1)} %bitcast.36), kind=kOutput, calls=%fused_computation.65 | convolution fusion | flops 25165824 | bytes 8407040 | tf_op jit(solution)/shard_map/dot_general | solution.py:49
  273.0 55.8 %psum.53 = f32[512]{0:T(512)S(1)} all-reduce(f32[512]{0:T(512)S(1)} %bitcast.42), channel_id=1, replica_groups=mesh['rows'=8,'protos'=32] {'protos'}, use_global_device_ids=true, to_apply=%region_8.0 | all-reduce | flops 512 | bytes 4096 | tf_op jit(solution)/shard_map/psum | solution.py:53
  328.8 6.5 fusion.17
  335.3 37.6 %psum.54 = f32[4096]{0:T(1024)} all-reduce(f32[4096]{0:T(1024)S(1)} %bitcast.37), channel_id=1, replica_groups=mesh['rows'=8,'protos'=32] {'rows'}, use_global_device_ids=true, to_apply=%region_9.0 | all-reduce | flops 4096 | bytes 32768 | tf_op jit(solution)/shard_map/psum | solution.py:48
  373.6 10.0 %fusion.18 = f32[1,512]{1,0:T(1,128)} fusion(f32[512,4096]{1,0:T(8,128)} %copy-done, f32[4096,1]{0,1:T(1,128)S(1)} %bitcast.33), kind=kOutput, calls=%fused_computation.67 | convolution fusion | flops 25165824 | bytes 8407040 | tf_op jit(solution)/shard_map/dot_general | solution.py:49
  383.7 6.2 fusion
  389.9 58.2 %all-reduce = (f32[512]{0:T(512)}, f32[512]{0:T(512)}) all-reduce(f32[512]{0:T(512)} %bitcast.39, f32[512]{0:T(512)} %get-tuple-element.4), channel_id=1, replica_groups=mesh['rows'=8,'protos'=32] {'protos'}, use_global_device_ids=true, to_apply=%region_10.0 | all-reduce | flops 1024 | bytes 8192 | tf_op jit(solution)/shard_map/psum | solution.py:53
  448.7 7.3 subtract_convert_fusion
  456.1 2.0 copy-done.2
  458.1 3.3 convolution_multiply_fusion.1
  461.5 7.2 convolution_multiply_fusion
  468.8 212.9 %reduce-scatter.3.cloned.1.call-done = f32[16,384]{1,0:T(8,128)} async-done(((f32[512,384]{1,0:T(8,128)}), f32[16,384]{1,0:T(8,128)}) %reduce-scatter.3.cloned.1.call-update) | async-done | bytes 24592 | tf_op jit(solution)/shard_map/reduce_scatter | solution.py:59
  681.6 51.1 %reduce-scatter.5.cloned.1.call-done = f32[1,512,384]{2,1,0:T(8,128)} async-done(((f32[8,512,384]{2,1,0:T(8,128)}), f32[1,512,384]{2,1,0:T(8,128)}) %reduce-scatter.5.cloned.1.call-update) | async-done | bytes 786448 | tf_op jit(solution)/shard_map/reduce_scatter | solution.py:67
  (33 shorter events, 15.0 us)
Async XLA Ops:
  52.1 331.5 %all-to-all-start = ((bf16[32,16,384]{2,1,0:T(8,128)(2,1)}), bf16[32,16,384]{2,1,0:T(8,128)(2,1)S(1)}, u32[]{:S(2)}, u32[]{:S(2)}) async-start(bf16[32,16,384]{2,1,0:T(8,128)(2,1)} %bitcast), calls=%async_computation | async-start | bytes 786432 | tf_op jit(solution)/shard_map/all_to_all | solution.py:15
  64.1 617.5 %reduce-scatter.3.cloned.1.call-start = ((), (), s32[]{:S(2)}) async-start(), calls=%async_computation.3 | async-start | bytes 811008 | tf_op jit(solution)/shard_map/reduce_scatter | solution.py:59
  68.4 50.4 %copy-start.3 = (f32[4096]{0:T(1024)}, f32[4096]{0:T(1024)S(1)}, u32[]{:S(2)}) copy-start(f32[4096]{0:T(1024)S(1)} %add_rsqrt_fusion) | copy-start | bytes 49156
  111.5 3.2 copy-start
  328.8 54.9 %copy-start.1 = (bf16[4096,384]{1,0:T(8,128)(2,1)S(1)}, bf16[4096,384]{1,0:T(8,128)(2,1)}, u32[]{:S(2)}) copy-start(bf16[4096,384]{1,0:T(8,128)(2,1)} %param.5) | copy-start | bytes 9437188
  448.7 9.4 %copy-start.4 = (f32[4096]{0:T(1024)S(1)}, f32[4096]{0:T(1024)}, u32[]{:S(2)}) copy-start(f32[4096]{0:T(1024)} %copy-done.3) | copy-start | bytes 49156
  456.1 2.0 copy-start.2
  461.5 271.3 %reduce-scatter.5.cloned.1.call-start = ((), (), s32[]{:S(2)}) async-start(), calls=%async_computation.4 | async-start | bytes 7077888 | tf_op jit(solution)/shard_map/reduce_scatter | solution.py:67
Sparse Core Ops, SparseCore 0:
  461.6 220.0 reduce-scatter.2
  684.8 47.9 reduce-scatter.4
